TPU v7x, 32 devices: a whole 2x2x4 slice. The times are simulated.
32 devices in a mesh: grp: 2 (over x), con: 16 (over z, y, core).
Axes of the slice: x: 2, y: 2, z: 4, core: 2. Of those that a mesh axis runs over, the one named last changes fastest.
Arguments:
- matrix: float32 [32768, 2048], P(('grp', 'con')), parts along dimension 0, may hold values from -0.046875 to 0.046875
- bounds_rhs: float32 [32768, 128], P(('grp', 'con')), parts along dimension 0, may hold values from -3 to 3
- costs: float32 [4096, 128], P(('grp', 'con')), parts along dimension 0, may hold values from -12 to 12
- upper: float32 [4096], P(('grp', 'con')), parts along dimension 0, may hold values from 0.5 to 2
- bound_mask: int32 [4096], P(('grp', 'con')), parts along dimension 0, may hold values 0 or 1
- node_map: int32 [3, 256], P(None, 'grp'), parts along dimension 1, may hold values from 0 to 63, as said below
- weights: int32 [256], P('grp'), parts along dimension 0, may hold values from 1 to 10
Outputs:
- primal: float32 [4096, 128], P(('grp', 'con')), parts along dimension 0
- dual: float32 [32768, 128], P(('grp', 'con')), parts along dimension 0
- multipliers: float32 [4096, 128], P(('grp', 'con')), parts along dimension 0
- gaps: float32 [4], P('grp'), parts along dimension 0
There are 2 independent parts, one for each index of `grp`. A program takes and returns all parts, laid end to end along the dimension named above; each array names one. Nothing has to cross between parts.
Inputs may be any that keep to these rules, and one draw needn't show every extreme that they name: `node_map`: row t numbers the 4 ** (t + 1) nodes of that section; each node holds 128 / 4 ** (t + 1) scenarios, and the nodes of row t + 1 split those of row t.
All inputs are finite; a program needn't handle non-finite values. No bound on the sum of `bound_mask` on one device may be relied on, other than what follows from the above.
Results may differ from a plain program's by a relative error of at most 0.0001.
Values sent between devices are 32-bit elements; how exact they have to be, the bound alone decides.
A program may use at most 64 MiB of HBM per device.

v0:
```python
import jax
import jax.numpy as jnp
from jax import lax
from jax.sharding import PartitionSpec as P

N = 2048
OUTER = 2
INNER = 2
highest = lax.Precision.HIGHEST
step_primal = 0.4
step_dual = 0.6
penalty = 1.0


def node_average(node_map, weights):
    weight_float = weights.astype(jnp.float32)
    probability = weight_float / jnp.sum(weight_float)
    same_node = (node_map[:, :, None] == node_map[:, None, :]).astype(jnp.float32)
    node_mass = same_node * probability[None, None, :]
    return (node_mass / jnp.sum(node_mass, axis=2, keepdims=True), probability)


def consensus(primal, averaging, column_index):
    averaged = jnp.einsum("tsr,jr->tjs", averaging, primal, precision=highest)
    section_of = column_index % (averaging.shape[0] + 1)
    section_hot = (
        section_of[None, :] == jnp.arange(averaging.shape[0], dtype=jnp.int32)[:, None]
    ).astype(jnp.float32)
    free_cols = 1.0 - jnp.sum(section_hot, axis=0)
    return jnp.sum(section_hot[:, :, None] * averaged, axis=0) + free_cols[:, None] * primal


def primal_step(primal, costs, multipliers, average, transposed, upper, flags, prox_weight):
    gradient = costs + multipliers + prox_weight * (primal - average) + transposed
    moved = jnp.maximum(primal - step_primal * gradient, 0.0)
    return jnp.where(flags[:, None] > 0, jnp.minimum(moved, upper[:, None]), moved)


def apply_rows(matrix, extrap):
    return jnp.dot(matrix, lax.all_gather(extrap, "con", axis=0, tiled=True), precision=highest)


def apply_columns(matrix, dual):
    return lax.psum_scatter(
        lax.dot_general(matrix, dual, (((0,), (0,)), ((), ())), precision=highest),
        "con",
        scatter_dimension=0,
        tiled=True,
    )


def body(matrix, bounds_rhs, costs, upper, bound_mask, node_map, weights):
    own_cols = costs.shape[0]
    scenario_count = costs.shape[1]
    averaging, probability = node_average(node_map, weights)
    start_col = lax.axis_index("con") * own_cols
    costs_all, upper_all, flags_all = (costs, upper, bound_mask.astype(jnp.float32))
    width = costs_all.shape[0]
    column_index = start_col + jnp.arange(width, dtype=jnp.int32)
    primal = jnp.zeros((width, scenario_count), jnp.float32)
    multipliers = jnp.zeros((width, scenario_count), jnp.float32)
    average = jnp.zeros((width, scenario_count), jnp.float32)
    transposed = jnp.zeros((width, scenario_count), jnp.float32)
    dual = jnp.zeros(bounds_rhs.shape, jnp.float32)
    partials = []
    for outer_turn in range(OUTER):
        prox_weight = 0.0 if outer_turn == 0 else penalty
        for inner_turn in range(INNER):
            moved = primal_step(
                primal,
                costs_all,
                multipliers,
                average,
                transposed,
                upper_all,
                flags_all,
                prox_weight,
            )
            extrap = 2.0 * moved - primal
            product = apply_rows(matrix, extrap)
            dual = jnp.maximum(dual + step_dual * (product - bounds_rhs), 0.0)
            primal = moved
            if outer_turn < OUTER - 1 or inner_turn < INNER - 1:
                transposed = apply_columns(matrix, dual)
        average = consensus(primal, averaging, column_index)
        deviation = primal - average
        multipliers = multipliers + penalty * deviation
        partial_value = jnp.sum(deviation * deviation * probability[None, :]) / N
        partial_value = lax.psum(partial_value, "con")
        partials.append(partial_value)
    gaps = jnp.stack(partials)
    return (primal, dual, multipliers, gaps)


def solution(mesh):
    placed = (
        P(("grp", "con"), None),
        P(("grp", "con"), None),
        P(("grp", "con"), None),
        P(("grp", "con")),
        P(("grp", "con")),
        P(None, "grp"),
        P("grp"),
    )
    return jax.shard_map(
        body,
        mesh=mesh,
        in_specs=placed,
        out_specs=(
            P(("grp", "con"), None),
            P(("grp", "con"), None),
            P(("grp", "con"), None),
            P("grp"),
        ),
        check_vma=False,
    )
```

profile of v0, /device:TPU:0, one launch (start us, length us, event | category | flops | bytes accessed | tf_op | source)
XLA Modules:
  0.0 413.3 jit_solution(4604648816111772595)
XLA Ops:
  7.2 0.0 all-gather.5.cloned.1.call-start
  7.2 0.7 convert_compare_fusion
  7.9 0.9 copy.23
  8.8 1.3 fusion.31
  10.1 0.0 all-gather.5.cloned.1.call-update
  10.1 0.0 reduce-scatter.4.cloned.1.call-start
  10.2 1.2 copy.25
  11.4 0.0 copy-start.2
  11.4 38.8 %all-gather.5.cloned.1.call-done = f32[2048,128]{0,1:T(8,128)} async-done(((f32[128,128]{0,1:T(8,128)}), f32[2048,128]{0,1:T(8,128)}) %all-gather.5.cloned.1.call-update) | async-done | bytes 1048592 | tf_op jit(solution)/shard_map/all_gather | solution.py:40
  50.3 0.0 copy-start
  50.3 12.0 %fusion.8 = f32[1024,128]{0,1:T(8,128)S(1)} fusion(f32[1024,128]{0,1:T(8,128)S(1)} %copy.25, f32[2048,128]{0,1:T(8,128)} %all-gather.5.cloned.1.call-done, f32[1024,2048]{1,0:T(8,128)} %param.7), kind=kOutput, calls=%fused_computation.15 | convolution fusion | flops 3221618688 | bytes 10485760 | tf_op jit(solution)/shard_map/dot_general | solution.py:40
  62.3 0.0 copy-done
  62.3 5.6 %convolution_bitcast_fusion.2 = f32[2048,128]{0,1:T(8,128)} fusion(f32[1024,128]{0,1:T(8,128)S(1)} %fusion.8, f32[1024,2048]{1,0:T(8,128)S(1)} %copy-done), kind=kOutput, calls=%fused_computation.2 | convolution fusion | flops 3221225472 | bytes 9961472 | tf_op jit(solution)/shard_map/dot_general | solution.py:45
  67.8 0.0 reduce-scatter.4.cloned.1.call-update
  67.9 0.0 all-gather.7.cloned.1.call-start
  67.9 57.0 %reduce-scatter.4.cloned.1.call-done = f32[128,128]{0,1:T(8,128)} async-done(((f32[2048,128]{0,1:T(8,128)}), f32[128,128]{0,1:T(8,128)}) %reduce-scatter.4.cloned.1.call-update) | async-done | bytes 65552 | tf_op jit(solution)/shard_map/reduce_scatter | solution.py:44
  124.9 0.0 copy-done.2
  124.9 1.5 multiply_subtract_fusion.2
  126.5 0.0 all-gather.7.cloned.1.call-update
  126.5 0.0 copy-start.3
  126.5 0.0 copy-start.1
  126.5 0.2 reduce-scatter.6.cloned.1.call-start
  126.7 37.0 %all-gather.7.cloned.1.call-done = f32[2048,128]{0,1:T(8,128)} async-done(((f32[128,128]{0,1:T(8,128)}), f32[2048,128]{0,1:T(8,128)}) %all-gather.7.cloned.1.call-update) | async-done | bytes 1048592 | tf_op jit(solution)/shard_map/all_gather | solution.py:40
  163.7 11.5 %fusion.10 = f32[1024,128]{0,1:T(8,128)S(1)} fusion(f32[1024,128]{0,1:T(8,128)S(1)} %fusion.8, f32[1024,128]{0,1:T(8,128)S(1)} %copy.25, f32[2048,128]{0,1:T(8,128)} %all-gather.7.cloned.1.call-done, f32[1024,2048]{1,0:T(8,128)} %param.7), kind=kOutput, calls=%fused_computation.17 | convolution fusion | flops 3221749760 | bytes 11010048 | tf_op jit(solution)/shard_map/dot_general | solution.py:40
  175.2 7.8 %convolution_bitcast_fusion.1 = f32[2048,128]{0,1:T(8,128)} fusion(f32[1024,128]{0,1:T(8,128)S(1)} %fusion.10, f32[1024,2048]{1,0:T(8,128)} %param.7), kind=kOutput, calls=%fused_computation.1 | convolution fusion | flops 3221225472 | bytes 9961472 | tf_op jit(solution)/shard_map/dot_general | solution.py:45
  183.0 0.0 reduce-scatter.6.cloned.1.call-update
  183.1 0.0 all-gather.9.cloned.1.call-start
  183.1 0.0 copy-done.3
  183.1 0.6 convert_reduce_fusion
  183.8 0.6 convert_divide_fusion
  184.4 0.0 copy-done.1
  184.4 0.2 select_reduce_fusion
  184.7 0.5 fusion.17
  185.2 0.1 copy.27
  185.3 54.8 %reduce-scatter.6.cloned.1.call-done = f32[128,128]{0,1:T(8,128)} async-done(((f32[2048,128]{0,1:T(8,128)}), f32[128,128]{0,1:T(8,128)}) %reduce-scatter.6.cloned.1.call-update) | async-done | bytes 65552 | tf_op jit(solution)/shard_map/reduce_scatter | solution.py:44
  240.1 1.5 multiply_subtract_fusion.1
  241.6 0.0 all-gather.9.cloned.1.call-update
  241.6 0.3 reduce-scatter.8.cloned.1.call-start
  241.9 36.7 %all-gather.9.cloned.1.call-done = f32[2048,128]{0,1:T(8,128)} async-done(((f32[128,128]{0,1:T(8,128)}), f32[2048,128]{0,1:T(8,128)}) %all-gather.9.cloned.1.call-update) | async-done | bytes 1048592 | tf_op jit(solution)/shard_map/all_gather | solution.py:40
  278.6 11.4 %fusion.12 = f32[1024,128]{0,1:T(8,128)S(1)} fusion(f32[1024,128]{0,1:T(8,128)S(1)} %fusion.10, f32[1024,128]{0,1:T(8,128)S(1)} %copy.25, f32[2048,128]{0,1:T(8,128)} %all-gather.9.cloned.1.call-done, f32[1024,2048]{1,0:T(8,128)} %param.7), kind=kOutput, calls=%fused_computation.19 | convolution fusion | flops 3221749760 | bytes 11010048 | tf_op jit(solution)/shard_map/dot_general | solution.py:40
  290.0 7.8 %convolution_bitcast_fusion = f32[2048,128]{0,1:T(8,128)} fusion(f32[1024,128]{0,1:T(8,128)S(1)} %fusion.12, f32[1024,2048]{1,0:T(8,128)} %param.7), kind=kOutput, calls=%fused_computation | convolution fusion | flops 3221225472 | bytes 9961472 | tf_op jit(solution)/shard_map/dot_general | solution.py:45
  297.9 0.0 reduce-scatter.8.cloned.1.call-update
  297.9 0.0 all-gather.11.cloned.1.call-start
  297.9 57.0 %reduce-scatter.8.cloned.1.call-done = f32[128,128]{0,1:T(8,128)} async-done(((f32[2048,128]{0,1:T(8,128)}), f32[128,128]{0,1:T(8,128)}) %reduce-scatter.8.cloned.1.call-update) | async-done | bytes 65552 | tf_op jit(solution)/shard_map/reduce_scatter | solution.py:44
  355.0 1.5 multiply_subtract_fusion
  356.5 0.0 all-gather.11.cloned.1.call-update
  356.5 0.5 fusion.18
  357.0 0.1 copy.33
  357.1 0.7 multiply_reduce_fusion.1
  359.1 31.6 %all-reduce = (f32[1]{0:T(128)}, f32[1]{0:T(128)}) all-reduce(f32[1]{0:T(128)} %bitcast.12, f32[1]{0:T(128)} %bitcast.11), channel_id=1, replica_groups=mesh['grp'=2,'con'=16] {'con'}, use_global_device_ids=true, to_apply=%region_11.12 | all-reduce | flops 2 | bytes 16 | tf_op jit(solution)/shard_map/psum | solution.py:89
  390.7 0.7 copy.34
  391.4 0.7 copy.36
  392.2 1.8 pad_maximum_fusion
  394.0 0.0 all-gather.11.cloned.1.call-done
  394.0 11.5 %fusion.14 = f32[1024,128]{0,1:T(8,128)S(1)} fusion(f32[1024,128]{0,1:T(8,128)S(1)} %fusion.12, f32[1024,128]{0,1:T(8,128)S(1)} %copy.25, f32[2048,128]{0,1:T(8,128)} %all-gather.11.cloned.1.call-done, f32[1024,2048]{1,0:T(8,128)} %param.7), kind=kOutput, calls=%fused_computation.21 | convolution fusion | flops 3221749760 | bytes 11010048 | tf_op jit(solution)/shard_map/dot_general | solution.py:40
  405.5 1.0 copy.35
  (4 shorter events, 0.0 us)
Async XLA Ops:
  7.2 43.1 %all-gather.5.cloned.1.call-start = ((), (), s32[]{:S(2)}) async-start(), calls=%async_computation.3 | async-start | bytes 1114112 | tf_op jit(solution)/shard_map/all_gather | solution.py:40
  10.1 114.8 %reduce-scatter.4.cloned.1.call-start = ((), (), s32[]{:S(2)}) async-start(), calls=%async_computation.4 | async-start | bytes 1114112 | tf_op jit(solution)/shard_map/reduce_scatter | solution.py:44
  11.4 113.5 %copy-start.2 = (f32[128]{0:T(128)S(1)}, f32[128]{0:T(128)}, u32[]{:S(2)}) copy-start(f32[128]{0:T(128)} %param.10) | copy-start | bytes 1540
  50.3 12.0 %copy-start = (f32[1024,2048]{1,0:T(8,128)S(1)}, f32[1024,2048]{1,0:T(8,128)}, u32[]{:S(2)}) copy-start(f32[1024,2048]{1,0:T(8,128)} %param.7) | copy-start | bytes 25165828
  67.9 95.9 %all-gather.7.cloned.1.call-start = ((), (), s32[]{:S(2)}) async-start(), calls=%async_computation.5 | async-start | bytes 1114112 | tf_op jit(solution)/shard_map/all_gather | solution.py:40
  126.5 56.7 %copy-start.3 = (s32[128]{0:T(128)S(1)}, s32[128]{0:T(128)}, u32[]{:S(2)}) copy-start(s32[128]{0:T(128)} %param.13) | copy-start | bytes 1540
  126.5 57.9 %copy-start.1 = (s32[3,128]{1,0:T(4,128)S(1)}, s32[3,128]{1,0:T(4,128)}, u32[]{:S(2)}) copy-start(s32[3,128]{1,0:T(4,128)} %param.12) | copy-start | bytes 4612
  126.5 113.6 %reduce-scatter.6.cloned.1.call-start = ((), (), s32[]{:S(2)}) async-start(), calls=%async_computation.6 | async-start | bytes 1114112 | tf_op jit(solution)/shard_map/reduce_scatter | solution.py:44
  183.1 95.5 %all-gather.9.cloned.1.call-start = ((), (), s32[]{:S(2)}) async-start(), calls=%async_computation.7 | async-start | bytes 1114112 | tf_op jit(solution)/shard_map/all_gather | solution.py:40
  241.6 113.4 %reduce-scatter.8.cloned.1.call-start = ((), (), s32[]{:S(2)}) async-start(), calls=%async_computation.8 | async-start | bytes 1114112 | tf_op jit(solution)/shard_map/reduce_scatter | solution.py:44
  297.9 96.1 %all-gather.11.cloned.1.call-start = ((), (), s32[]{:S(2)}) async-start(), calls=%async_computation.9 | async-start | bytes 1114112 | tf_op jit(solution)/shard_map/all_gather | solution.py:40
Sparse Core Ops, SparseCore 0:
  10.7 39.4 all-gather.4
  68.0 56.8 reduce-scatter.3
  127.9 35.7 all-gather.6
  183.2 56.8 reduce-scatter.5
  242.7 35.8 all-gather.8
  298.0 56.9 reduce-scatter.7
  357.9 35.7 all-gather.10
where the time goes:
time: 414 us; the launch traced here: 413 us
  waiting for transfers between devices  281 us (68%)
  matrix products  68.6 us (17%)
  blocking collectives  31.6 us (8%)
  between operations  15.6 us (4%)
  other arithmetic  10.5 us (3%)
  local copies, waits for them, and re-layouts  4.82 us (1%)
    reduce_scatter x3, waiting for transfers between devices, apply_columns(): lax.psum_scatter(lax.dot_general(matrix, dual, (((0,), (0,)), ((), ())),...  169 us
    all_gather x4, waiting for transfers between devices, apply_rows(): lax.all_gather(extrap, 'con', axis=0, tiled=True)  112 us
    dot_general x4, matrix products, apply_rows(): jnp.dot(matrix, lax.all_gather(extrap, 'con', axis=0, tiled=True), precis...  46.3 us
    psum x1, blocking collectives, body(): partial_value = lax.psum(partial_value, 'con')  31.6 us
    dot_general x3, matrix products, apply_columns(): lax.dot_general(matrix, dual, (((0,), (0,)), ((), ())), precision=highest)  21.3 us
  transfers between devices with their start and end apart: 7, of which 6 were waited for; matrix products, arithmetic and copies ran while one was open for 2% of the time, Pallas kernels for 0%

commit v1 on v0

--- a/solution.py
+++ b/solution.py
@@ -10,6 +10,28 @@
 step_primal = 0.4
 step_dual = 0.6
 penalty = 1.0
+
+
+def laid_out(blocks, dim):
+    shape = list(blocks.shape[1:])
+    shape[dim] *= blocks.shape[0]
+    return jnp.moveaxis(blocks, 0, dim).reshape(shape)
+
+
+def collect(shard, axis, dim):
+    size = lax.axis_size(axis)
+    pairs = [(i, (i + 1) % size) for i in range(size)]
+    back = [(b, a) for a, b in pairs]
+    lower, upper = ([], [])
+    for step in range(size - 1):
+        if step % 2 == 0:
+            lower.append(lax.ppermute(lower[-1] if lower else shard, axis, pairs))
+        else:
+            upper.append(lax.ppermute(upper[-1] if upper else shard, axis, back))
+    pieces = jnp.stack([*lower[::-1], shard, *upper])
+    shift = lax.axis_index(axis) - len(lower)
+    pieces = pieces[(jnp.arange(size) - shift) % size]
+    return laid_out(pieces, dim)
 
 
 def node_average(node_map, weights):
@@ -37,7 +59,7 @@
 
 
 def apply_rows(matrix, extrap):
-    return jnp.dot(matrix, lax.all_gather(extrap, "con", axis=0, tiled=True), precision=highest)
+    return jnp.dot(matrix, collect(extrap, "con", 0), precision=highest)
 
 
 def apply_columns(matrix, dual):

time: 414 us -> 513 us (1.24)
  starting transfers between devices: 0.69 us -> 122 us
  waiting for transfers between devices: 281 us -> 247 us
  local copies, waits for them, and re-layouts: 4.82 us -> 21.2 us
  matrix products: 68.6 us -> 63.1 us
    ppermute x0 -> x60, starting transfers between devices: none -> 122 us  [the longest x28 120 us: collect(): upper.append(lax.ppermute(upper[-1] if upper else shard, axis, back))]
    all_gather x4 -> x0, waiting for transfers between devices: 112 us -> none  [apply_rows(): lax.all_gather(extrap, 'con', axis=0, tiled=True)]
    ppermute x0 -> x60, waiting for transfers between devices: none -> 76.5 us  [the longest x32 72.1 us: collect(): lower.append(lax.ppermute(lower[-1] if lower else shard, axis, pairs))]
    unnamed x13 -> x70, local copies, waits for them, and re-layouts: 4.64 us -> 14.4 us
    dot_general x4, matrix products: 46.3 us -> 38.5 us  [apply_rows(): return jnp.dot(matrix, collect(extrap, 'con', 0), precision=highest)]
    gather x0 -> x8, local copies, waits for them, and re-layouts: none -> 6 us  [collect(): pieces = pieces[(jnp.arange(size) - shift) % size]]
  transfers between devices with their start and end apart: 7 -> 63, of which waited for: 6 -> 38; matrix products, arithmetic and copies ran while one was open for 2% -> 4% of each run, Pallas kernels for 0% -> 0%
where the time goes in v1:
time: 513 us
  waiting for transfers between devices  247 us (48%)
  starting transfers between devices  122 us (24%)
  matrix products  63.1 us (12%)
  blocking collectives  35.7 us (7%)
  local copies, waits for them, and re-layouts  21.2 us (4%)
  between operations  15.7 us (3%)
  other arithmetic  8.7 us (2%)
    reduce_scatter x3, waiting for transfers between devices, apply_columns(): lax.psum_scatter(lax.dot_general(matrix, dual, (((0,), (0,)), ((), ())),...  170 us
    ppermute x28, starting transfers between devices, collect(): upper.append(lax.ppermute(upper[-1] if upper else shard, axis, back))  120 us
    ppermute x32, waiting for transfers between devices, collect(): lower.append(lax.ppermute(lower[-1] if lower else shard, axis, pairs))  72.1 us
    dot_general x4, matrix products, apply_rows(): return jnp.dot(matrix, collect(extrap, 'con', 0), precision=highest)  38.5 us
    psum x1, blocking collectives, body(): partial_value = lax.psum(partial_value, 'con')  35.7 us
    dot_general x3, matrix products, apply_columns(): lax.dot_general(matrix, dual, (((0,), (0,)), ((), ())), precision=highest)  23.5 us
    unnamed x70, local copies, waits for them, and re-layouts  14.4 us
  transfers between devices with their start and end apart: 63, of which 38 were waited for; matrix products, arithmetic and copies ran while one was open for 4% of the time, Pallas kernels for 0%

profile of v1, /device:TPU:0, one launch (start us, length us, event | category | flops | bytes accessed | tf_op | source)
XLA Modules:
  0.0 512.8 jit_solution(6232304768342384563)
XLA Ops:
  10.0 6.9 %collective-permute-done = f32[128,128]{0,1:T(8,128)S(1)} collective-permute-done((f32[128,128]{0,1:T(8,128)S(1)}, f32[128,128]{0,1:T(8,128)S(1)}, u32[]{:S(2)}, u32[]{:S(2)}) %collective-permute-start) | collective-permute-done | bytes 65568 | tf_op jit(solution)/shard_map/ppermute | solution.py:28
  16.9 4.4 collective-permute-start.8
  21.4 2.0 collective-permute-done.1
  23.3 4.4 collective-permute-start.9
  27.8 1.9 collective-permute-done.2
  29.7 4.5 collective-permute-start.10
  34.2 1.9 collective-permute-done.3
  36.1 4.5 collective-permute-start.11
  40.6 1.9 collective-permute-done.4
  43.8 4.5 collective-permute-start.12
  50.2 4.5 collective-permute-start.13
  56.6 4.5 collective-permute-start.14
  64.0 9.5 %fusion.8 = f32[1024,128]{0,1:T(8,128)S(1)} fusion(f32[1024,128]{0,1:T(8,128)S(1)} %copy.42, f32[2048,128]{1,0:T(8,128)S(1)} %bitcast.212, f32[1024,2048]{1,0:T(8,128)} %param.7), kind=kOutput, calls=%fused_computation.19 | convolution fusion | flops 3221618688 | bytes 10485760 | tf_op jit(solution)/shard_map/dot_general | solution.py:62
  73.5 7.8 %convolution_bitcast_fusion.2 = f32[2048,128]{0,1:T(8,128)} fusion(f32[1024,128]{0,1:T(8,128)S(1)} %fusion.8, f32[1024,2048]{1,0:T(8,128)} %param.7), kind=kOutput, calls=%fused_computation.6 | convolution fusion | flops 3221225472 | bytes 9961472 | tf_op jit(solution)/shard_map/dot_general | solution.py:67
  81.4 59.2 %reduce-scatter.4.cloned.1.call-done = f32[128,128]{0,1:T(8,128)} async-done(((f32[2048,128]{0,1:T(8,128)}), f32[128,128]{0,1:T(8,128)}) %reduce-scatter.4.cloned.1.call-update) | async-done | bytes 65552 | tf_op jit(solution)/shard_map/reduce_scatter | solution.py:66
  141.6 6.4 %collective-permute-done.15 = f32[128,128]{0,1:T(8,128)S(1)} collective-permute-done((f32[128,128]{0,1:T(8,128)S(1)}, f32[128,128]{0,1:T(8,128)S(1)}, u32[]{:S(2)}, u32[]{:S(2)}) %collective-permute-start.15) | collective-permute-done | bytes 65568 | tf_op jit(solution)/shard_map/ppermute | solution.py:28
  148.0 4.4 collective-permute-start.23
  152.4 2.0 collective-permute-done.16
  154.5 4.4 collective-permute-start.24
  158.9 1.9 collective-permute-done.17
  160.9 4.5 collective-permute-start.25
  165.4 1.9 collective-permute-done.18
  167.3 4.5 collective-permute-start.26
  171.7 1.9 collective-permute-done.19
  173.7 4.5 collective-permute-start.27
  178.1 1.9 collective-permute-done.20
  180.0 4.5 collective-permute-start.28
  184.5 1.9 collective-permute-done.21
  186.4 4.5 collective-permute-start.29
  190.9 1.9 collective-permute-done.22
  194.0 9.6 %fusion.10 = f32[1024,128]{0,1:T(8,128)S(1)} fusion(f32[1024,128]{0,1:T(8,128)S(1)} %fusion.8, f32[1024,128]{0,1:T(8,128)S(1)} %copy.42, f32[2048,128]{1,0:T(8,128)S(1)} %bitcast.214, f32[1024,2048]{1,0:T(8,128)} %param.7), kind=kOutput, calls=%fused_computation.21 | convolution fusion | flops 3221749760 | bytes 11010048 | tf_op jit(solution)/shard_map/dot_general | solution.py:62
  203.6 7.8 %convolution_bitcast_fusion.1 = f32[2048,128]{0,1:T(8,128)} fusion(f32[1024,128]{0,1:T(8,128)S(1)} %fusion.10, f32[1024,2048]{1,0:T(8,128)} %param.7), kind=kOutput, calls=%fused_computation.5 | convolution fusion | flops 3221225472 | bytes 9961472 | tf_op jit(solution)/shard_map/dot_general | solution.py:67
  213.7 56.2 %reduce-scatter.6.cloned.1.call-done = f32[128,128]{0,1:T(8,128)} async-done(((f32[2048,128]{0,1:T(8,128)}), f32[128,128]{0,1:T(8,128)}) %reduce-scatter.6.cloned.1.call-update) | async-done | bytes 65552 | tf_op jit(solution)/shard_map/reduce_scatter | solution.py:66
  270.9 6.4 %collective-permute-done.30 = f32[128,128]{0,1:T(8,128)S(1)} collective-permute-done((f32[128,128]{0,1:T(8,128)S(1)}, f32[128,128]{0,1:T(8,128)S(1)}, u32[]{:S(2)}, u32[]{:S(2)}) %collective-permute-start.30) | collective-permute-done | bytes 65568 | tf_op jit(solution)/shard_map/ppermute | solution.py:28
  277.3 4.4 collective-permute-start.38
  281.7 2.0 collective-permute-done.31
  283.8 4.4 collective-permute-start.39
  288.2 1.9 collective-permute-done.32
  290.1 4.5 collective-permute-start.40
  294.6 1.9 collective-permute-done.33
  296.6 4.5 collective-permute-start.41
  301.0 1.9 collective-permute-done.34
  302.9 4.5 collective-permute-start.42
  307.4 1.9 collective-permute-done.35
  309.3 4.5 collective-permute-start.43
  313.8 1.9 collective-permute-done.36
  315.7 4.5 collective-permute-start.44
  320.2 1.9 collective-permute-done.37
  335.3 9.9 %fusion.12 = f32[1024,128]{0,1:T(8,128)S(1)} fusion(f32[1024,128]{0,1:T(8,128)S(1)} %fusion.10, f32[1024,128]{0,1:T(8,128)S(1)} %copy.42, f32[2048,128]{1,0:T(8,128)} %bitcast.215, f32[1024,2048]{1,0:T(8,128)} %param.7), kind=kOutput, calls=%fused_computation.23 | convolution fusion | flops 3221749760 | bytes 11010048 | tf_op jit(solution)/shard_map/dot_general | solution.py:62
  345.2 7.8 %convolution_bitcast_fusion = f32[2048,128]{0,1:T(8,128)} fusion(f32[1024,128]{0,1:T(8,128)S(1)} %fusion.12, f32[1024,2048]{1,0:T(8,128)} %param.7), kind=kOutput, calls=%fused_computation.4 | convolution fusion | flops 3221225472 | bytes 9961472 | tf_op jit(solution)/shard_map/dot_general | solution.py:67
  353.1 54.8 %reduce-scatter.8.cloned.1.call-done = f32[128,128]{0,1:T(8,128)} async-done(((f32[2048,128]{0,1:T(8,128)}), f32[128,128]{0,1:T(8,128)}) %reduce-scatter.8.cloned.1.call-update) | async-done | bytes 65552 | tf_op jit(solution)/shard_map/reduce_scatter | solution.py:66
  408.8 6.4 %collective-permute-done.45 = f32[128,128]{0,1:T(8,128)S(1)} collective-permute-done((f32[128,128]{0,1:T(8,128)S(1)}, f32[128,128]{0,1:T(8,128)S(1)}, u32[]{:S(2)}, u32[]{:S(2)}) %collective-permute-start.45) | collective-permute-done | bytes 65568 | tf_op jit(solution)/shard_map/ppermute | solution.py:28
  415.2 4.4 collective-permute-start.53
  419.6 2.0 collective-permute-done.46
  421.7 4.4 collective-permute-start.54
  426.1 1.9 collective-permute-done.47
  428.1 4.5 collective-permute-start.55
  432.6 1.9 collective-permute-done.48
  434.5 4.5 collective-permute-start.56
  439.0 2.0 collective-permute-done.49
  441.6 4.5 collective-permute-start.57
  449.3 35.7 %all-reduce = (f32[1]{0:T(128)}, f32[1]{0:T(128)}) all-reduce(f32[1]{0:T(128)} %bitcast.81, f32[1]{0:T(128)} %bitcast.80), channel_id=1, replica_groups=mesh['grp'=2,'con'=16] {'con'}, use_global_device_ids=true, to_apply=%region_11.12 | all-reduce | flops 2 | bytes 16 | tf_op jit(solution)/shard_map/psum | solution.py:111
  488.8 4.0 collective-permute-start.59
  495.7 9.6 %fusion.14 = f32[1024,128]{0,1:T(8,128)S(1)} fusion(f32[1024,128]{0,1:T(8,128)S(1)} %fusion.12, f32[1024,128]{0,1:T(8,128)S(1)} %copy.42, f32[2048,128]{1,0:T(8,128)S(1)} %bitcast.213, f32[1024,2048]{1,0:T(8,128)} %param.7), kind=kOutput, calls=%fused_computation.25 | convolution fusion | flops 3221749760 | bytes 11010048 | tf_op jit(solution)/shard_map/dot_general | solution.py:62
  (176 shorter events, 40.4 us)
Async XLA Ops:
  7.2 133.5 %reduce-scatter.4.cloned.1.call-start = ((), (), s32[]{:S(2)}) async-start(), calls=%async_computation.3 | async-start | bytes 1114112 | tf_op jit(solution)/shard_map/reduce_scatter | solution.py:66
  9.5 7.4 %collective-permute-start = (f32[128,128]{0,1:T(8,128)S(1)}, f32[128,128]{0,1:T(8,128)S(1)}, u32[]{:S(2)}, u32[]{:S(2)}) collective-permute-start(f32[128,128]{0,1:T(8,128)S(1)} %fusion.31), channel_id=1, source_target_pairs={{0,1},{1,2},{2,3},{3,4},{4,5},{5,6},{6,7},{7,8},{8,9},{9,10},{10,1... | collective-permute-start | bytes 196616 | tf_op jit(solution)/shard_map/ppermute | solution.py:28
  16.9 6.4 %collective-permute-start.1 = (f32[128,128]{0,1:T(8,128)S(1)}, f32[128,128]{0,1:T(8,128)S(1)}, u32[]{:S(2)}, u32[]{:S(2)}) collective-permute-start(f32[128,128]{0,1:T(8,128)S(1)} %collective-permute-done), channel_id=1, source_target_pairs={{0,1},{1,2},{2,3},{3,4},{4,5},{5,6},{6,7},{7,8},{8,9},{9,10},{10,1... | collective-permute-start | bytes 196616 | tf_op jit(solution)/shard_map/ppermute | solution.py:28
  16.9 6.4 %collective-permute-start.8 = (f32[128,128]{0,1:T(8,128)S(1)}, f32[128,128]{0,1:T(8,128)S(1)}, u32[]{:S(2)}, u32[]{:S(2)}) collective-permute-start(f32[128,128]{0,1:T(8,128)S(1)} %fusion.31), channel_id=1, source_target_pairs={{1,0},{2,1},{3,2},{4,3},{5,4},{6,5},{7,6},{8,7},{9,8},{10,9},{11,1... | collective-permute-start | bytes 196616 | tf_op jit(solution)/shard_map/ppermute | solution.py:30
  23.3 6.4 %collective-permute-start.2 = (f32[128,128]{0,1:T(8,128)S(1)}, f32[128,128]{0,1:T(8,128)S(1)}, u32[]{:S(2)}, u32[]{:S(2)}) collective-permute-start(f32[128,128]{0,1:T(8,128)S(1)} %collective-permute-done.1), channel_id=1, source_target_pairs={{0,1},{1,2},{2,3},{3,4},{4,5},{5,6},{6,7},{7,8},{8,9},{9,10},{10,1... | collective-permute-start | bytes 196616 | tf_op jit(solution)/shard_map/ppermute | solution.py:28
  23.3 6.4 %collective-permute-start.9 = (f32[128,128]{0,1:T(8,128)S(1)}, f32[128,128]{0,1:T(8,128)S(1)}, u32[]{:S(2)}, u32[]{:S(2)}) collective-permute-start(f32[128,128]{0,1:T(8,128)S(1)} %collective-permute-done.8), channel_id=1, source_target_pairs={{1,0},{2,1},{3,2},{4,3},{5,4},{6,5},{7,6},{8,7},{9,8},{10,9},{11,1... | collective-permute-start | bytes 196616 | tf_op jit(solution)/shard_map/ppermute | solution.py:30
  29.7 6.4 %collective-permute-start.3 = (f32[128,128]{0,1:T(8,128)S(1)}, f32[128,128]{0,1:T(8,128)S(1)}, u32[]{:S(2)}, u32[]{:S(2)}) collective-permute-start(f32[128,128]{0,1:T(8,128)S(1)} %collective-permute-done.2), channel_id=1, source_target_pairs={{0,1},{1,2},{2,3},{3,4},{4,5},{5,6},{6,7},{7,8},{8,9},{9,10},{10,1... | collective-permute-start | bytes 196616 | tf_op jit(solution)/shard_map/ppermute | solution.py:28
  29.7 6.4 %collective-permute-start.10 = (f32[128,128]{0,1:T(8,128)S(1)}, f32[128,128]{0,1:T(8,128)S(1)}, u32[]{:S(2)}, u32[]{:S(2)}) collective-permute-start(f32[128,128]{0,1:T(8,128)S(1)} %collective-permute-done.9), channel_id=1, source_target_pairs={{1,0},{2,1},{3,2},{4,3},{5,4},{6,5},{7,6},{8,7},{9,8},{10,9},{11,1... | collective-permute-start | bytes 196616 | tf_op jit(solution)/shard_map/ppermute | solution.py:30
  36.1 6.5 %collective-permute-start.4 = (f32[128,128]{0,1:T(8,128)S(1)}, f32[128,128]{0,1:T(8,128)S(1)}, u32[]{:S(2)}, u32[]{:S(2)}) collective-permute-start(f32[128,128]{0,1:T(8,128)S(1)} %collective-permute-done.3), channel_id=1, source_target_pairs={{0,1},{1,2},{2,3},{3,4},{4,5},{5,6},{6,7},{7,8},{8,9},{9,10},{10,1... | collective-permute-start | bytes 196616 | tf_op jit(solution)/shard_map/ppermute | solution.py:28
  36.1 7.7 %collective-permute-start.11 = (f32[128,128]{0,1:T(8,128)S(1)}, f32[128,128]{0,1:T(8,128)S(1)}, u32[]{:S(2)}, u32[]{:S(2)}) collective-permute-start(f32[128,128]{0,1:T(8,128)S(1)} %collective-permute-done.10), channel_id=1, source_target_pairs={{1,0},{2,1},{3,2},{4,3},{5,4},{6,5},{7,6},{8,7},{9,8},{10,9},{11,1... | collective-permute-start | bytes 196616 | tf_op jit(solution)/shard_map/ppermute | solution.py:30
  42.6 6.4 %collective-permute-start.5 = (f32[128,128]{0,1:T(8,128)S(1)}, f32[128,128]{0,1:T(8,128)S(1)}, u32[]{:S(2)}, u32[]{:S(2)}) collective-permute-start(f32[128,128]{0,1:T(8,128)S(1)} %collective-permute-done.4), channel_id=1, source_target_pairs={{0,1},{1,2},{2,3},{3,4},{4,5},{5,6},{6,7},{7,8},{8,9},{9,10},{10,1... | collective-permute-start | bytes 196616 | tf_op jit(solution)/shard_map/ppermute | solution.py:28
  43.8 6.4 %collective-permute-start.12 = (f32[128,128]{0,1:T(8,128)S(1)}, f32[128,128]{0,1:T(8,128)S(1)}, u32[]{:S(2)}, u32[]{:S(2)}) collective-permute-start(f32[128,128]{0,1:T(8,128)S(1)} %collective-permute-done.11), channel_id=1, source_target_pairs={{1,0},{2,1},{3,2},{4,3},{5,4},{6,5},{7,6},{8,7},{9,8},{10,9},{11,1... | collective-permute-start | bytes 196616 | tf_op jit(solution)/shard_map/ppermute | solution.py:30
  49.0 6.4 %collective-permute-start.6 = (f32[128,128]{0,1:T(8,128)S(1)}, f32[128,128]{0,1:T(8,128)S(1)}, u32[]{:S(2)}, u32[]{:S(2)}) collective-permute-start(f32[128,128]{0,1:T(8,128)S(1)} %collective-permute-done.5), channel_id=1, source_target_pairs={{0,1},{1,2},{2,3},{3,4},{4,5},{5,6},{6,7},{7,8},{8,9},{9,10},{10,1... | collective-permute-start | bytes 196616 | tf_op jit(solution)/shard_map/ppermute | solution.py:28
  50.2 6.4 %collective-permute-start.13 = (f32[128,128]{0,1:T(8,128)S(1)}, f32[128,128]{0,1:T(8,128)S(1)}, u32[]{:S(2)}, u32[]{:S(2)}) collective-permute-start(f32[128,128]{0,1:T(8,128)S(1)} %collective-permute-done.12), channel_id=1, source_target_pairs={{1,0},{2,1},{3,2},{4,3},{5,4},{6,5},{7,6},{8,7},{9,8},{10,9},{11,1... | collective-permute-start | bytes 196616 | tf_op jit(solution)/shard_map/ppermute | solution.py:30
  55.5 6.4 %collective-permute-start.7 = (f32[128,128]{0,1:T(8,128)S(1)}, f32[128,128]{0,1:T(8,128)S(1)}, u32[]{:S(2)}, u32[]{:S(2)}) collective-permute-start(f32[128,128]{0,1:T(8,128)S(1)} %collective-permute-done.6), channel_id=1, source_target_pairs={{0,1},{1,2},{2,3},{3,4},{4,5},{5,6},{6,7},{7,8},{8,9},{9,10},{10,1... | collective-permute-start | bytes 196616 | tf_op jit(solution)/shard_map/ppermute | solution.py:28
  56.6 6.4 %collective-permute-start.14 = (f32[128,128]{0,1:T(8,128)S(1)}, f32[128,128]{0,1:T(8,128)S(1)}, u32[]{:S(2)}, u32[]{:S(2)}) collective-permute-start(f32[128,128]{0,1:T(8,128)S(1)} %collective-permute-done.13), channel_id=1, source_target_pairs={{1,0},{2,1},{3,2},{4,3},{5,4},{6,5},{7,6},{8,7},{9,8},{10,9},{11,1... | collective-permute-start | bytes 196616 | tf_op jit(solution)/shard_map/ppermute | solution.py:30
  64.0 76.7 %copy-start = (f32[128]{0:T(128)S(1)}, f32[128]{0:T(128)}, u32[]{:S(2)}) copy-start(f32[128]{0:T(128)} %param.10) | copy-start | bytes 1540
  81.4 188.5 %reduce-scatter.6.cloned.1.call-start = ((), (), s32[]{:S(2)}) async-start(), calls=%async_computation.4 | async-start | bytes 1114112 | tf_op jit(solution)/shard_map/reduce_scatter | solution.py:66
  141.5 6.4 %collective-permute-start.15 = (f32[128,128]{0,1:T(8,128)S(1)}, f32[128,128]{0,1:T(8,128)S(1)}, u32[]{:S(2)}, u32[]{:S(2)}) collective-permute-start(f32[128,128]{0,1:T(8,128)S(1)} %get-tuple-element.26), channel_id=1, source_target_pairs={{0,1},{1,2},{2,3},{3,4},{4,5},{5,6},{6,7},{7,8},{8,9},{9,10},{10,1... | collective-permute-start | bytes 196616 | tf_op jit(solution)/shard_map/ppermute | solution.py:28
  148.0 6.5 %collective-permute-start.16 = (f32[128,128]{0,1:T(8,128)S(1)}, f32[128,128]{0,1:T(8,128)S(1)}, u32[]{:S(2)}, u32[]{:S(2)}) collective-permute-start(f32[128,128]{0,1:T(8,128)S(1)} %collective-permute-done.15), channel_id=1, source_target_pairs={{0,1},{1,2},{2,3},{3,4},{4,5},{5,6},{6,7},{7,8},{8,9},{9,10},{10,1... | collective-permute-start | bytes 196616 | tf_op jit(solution)/shard_map/ppermute | solution.py:28
  148.0 6.5 %collective-permute-start.23 = (f32[128,128]{0,1:T(8,128)S(1)}, f32[128,128]{0,1:T(8,128)S(1)}, u32[]{:S(2)}, u32[]{:S(2)}) collective-permute-start(f32[128,128]{0,1:T(8,128)S(1)} %get-tuple-element.26), channel_id=1, source_target_pairs={{1,0},{2,1},{3,2},{4,3},{5,4},{6,5},{7,6},{8,7},{9,8},{10,9},{11,1... | collective-permute-start | bytes 196616 | tf_op jit(solution)/shard_map/ppermute | solution.py:30
  154.5 6.4 %collective-permute-start.17 = (f32[128,128]{0,1:T(8,128)S(1)}, f32[128,128]{0,1:T(8,128)S(1)}, u32[]{:S(2)}, u32[]{:S(2)}) collective-permute-start(f32[128,128]{0,1:T(8,128)S(1)} %collective-permute-done.16), channel_id=1, source_target_pairs={{0,1},{1,2},{2,3},{3,4},{4,5},{5,6},{6,7},{7,8},{8,9},{9,10},{10,1... | collective-permute-start | bytes 196616 | tf_op jit(solution)/shard_map/ppermute | solution.py:28
  154.5 6.4 %collective-permute-start.24 = (f32[128,128]{0,1:T(8,128)S(1)}, f32[128,128]{0,1:T(8,128)S(1)}, u32[]{:S(2)}, u32[]{:S(2)}) collective-permute-start(f32[128,128]{0,1:T(8,128)S(1)} %collective-permute-done.23), channel_id=1, source_target_pairs={{1,0},{2,1},{3,2},{4,3},{5,4},{6,5},{7,6},{8,7},{9,8},{10,9},{11,1... | collective-permute-start | bytes 196616 | tf_op jit(solution)/shard_map/ppermute | solution.py:30
  160.9 6.4 %collective-permute-start.18 = (f32[128,128]{0,1:T(8,128)S(1)}, f32[128,128]{0,1:T(8,128)S(1)}, u32[]{:S(2)}, u32[]{:S(2)}) collective-permute-start(f32[128,128]{0,1:T(8,128)S(1)} %collective-permute-done.17), channel_id=1, source_target_pairs={{0,1},{1,2},{2,3},{3,4},{4,5},{5,6},{6,7},{7,8},{8,9},{9,10},{10,1... | collective-permute-start | bytes 196616 | tf_op jit(solution)/shard_map/ppermute | solution.py:28
  160.9 6.4 %collective-permute-start.25 = (f32[128,128]{0,1:T(8,128)S(1)}, f32[128,128]{0,1:T(8,128)S(1)}, u32[]{:S(2)}, u32[]{:S(2)}) collective-permute-start(f32[128,128]{0,1:T(8,128)S(1)} %collective-permute-done.24), channel_id=1, source_target_pairs={{1,0},{2,1},{3,2},{4,3},{5,4},{6,5},{7,6},{8,7},{9,8},{10,9},{11,1... | collective-permute-start | bytes 196616 | tf_op jit(solution)/shard_map/ppermute | solution.py:30
  167.2 6.4 %collective-permute-start.19 = (f32[128,128]{0,1:T(8,128)S(1)}, f32[128,128]{0,1:T(8,128)S(1)}, u32[]{:S(2)}, u32[]{:S(2)}) collective-permute-start(f32[128,128]{0,1:T(8,128)S(1)} %collective-permute-done.18), channel_id=1, source_target_pairs={{0,1},{1,2},{2,3},{3,4},{4,5},{5,6},{6,7},{7,8},{8,9},{9,10},{10,1... | collective-permute-start | bytes 196616 | tf_op jit(solution)/shard_map/ppermute | solution.py:28
  167.3 6.4 %collective-permute-start.26 = (f32[128,128]{0,1:T(8,128)S(1)}, f32[128,128]{0,1:T(8,128)S(1)}, u32[]{:S(2)}, u32[]{:S(2)}) collective-permute-start(f32[128,128]{0,1:T(8,128)S(1)} %collective-permute-done.25), channel_id=1, source_target_pairs={{1,0},{2,1},{3,2},{4,3},{5,4},{6,5},{7,6},{8,7},{9,8},{10,9},{11,1... | collective-permute-start | bytes 196616 | tf_op jit(solution)/shard_map/ppermute | solution.py:30
  173.6 6.4 %collective-permute-start.20 = (f32[128,128]{0,1:T(8,128)S(1)}, f32[128,128]{0,1:T(8,128)S(1)}, u32[]{:S(2)}, u32[]{:S(2)}) collective-permute-start(f32[128,128]{0,1:T(8,128)S(1)} %collective-permute-done.19), channel_id=1, source_target_pairs={{0,1},{1,2},{2,3},{3,4},{4,5},{5,6},{6,7},{7,8},{8,9},{9,10},{10,1... | collective-permute-start | bytes 196616 | tf_op jit(solution)/shard_map/ppermute | solution.py:28
  173.7 6.4 %collective-permute-start.27 = (f32[128,128]{0,1:T(8,128)S(1)}, f32[128,128]{0,1:T(8,128)S(1)}, u32[]{:S(2)}, u32[]{:S(2)}) collective-permute-start(f32[128,128]{0,1:T(8,128)S(1)} %collective-permute-done.26), channel_id=1, source_target_pairs={{1,0},{2,1},{3,2},{4,3},{5,4},{6,5},{7,6},{8,7},{9,8},{10,9},{11,1... | collective-permute-start | bytes 196616 | tf_op jit(solution)/shard_map/ppermute | solution.py:30
  180.0 6.4 %collective-permute-start.21 = (f32[128,128]{0,1:T(8,128)S(1)}, f32[128,128]{0,1:T(8,128)S(1)}, u32[]{:S(2)}, u32[]{:S(2)}) collective-permute-start(f32[128,128]{0,1:T(8,128)S(1)} %collective-permute-done.20), channel_id=1, source_target_pairs={{0,1},{1,2},{2,3},{3,4},{4,5},{5,6},{6,7},{7,8},{8,9},{9,10},{10,1... | collective-permute-start | bytes 196616 | tf_op jit(solution)/shard_map/ppermute | solution.py:28
  180.0 6.4 %collective-permute-start.28 = (f32[128,128]{0,1:T(8,128)S(1)}, f32[128,128]{0,1:T(8,128)S(1)}, u32[]{:S(2)}, u32[]{:S(2)}) collective-permute-start(f32[128,128]{0,1:T(8,128)S(1)} %collective-permute-done.27), channel_id=1, source_target_pairs={{1,0},{2,1},{3,2},{4,3},{5,4},{6,5},{7,6},{8,7},{9,8},{10,9},{11,1... | collective-permute-start | bytes 196616 | tf_op jit(solution)/shard_map/ppermute | solution.py:30
  186.4 6.4 %collective-permute-start.22 = (f32[128,128]{0,1:T(8,128)S(1)}, f32[128,128]{0,1:T(8,128)S(1)}, u32[]{:S(2)}, u32[]{:S(2)}) collective-permute-start(f32[128,128]{0,1:T(8,128)S(1)} %collective-permute-done.21), channel_id=1, source_target_pairs={{0,1},{1,2},{2,3},{3,4},{4,5},{5,6},{6,7},{7,8},{8,9},{9,10},{10,1... | collective-permute-start | bytes 196616 | tf_op jit(solution)/shard_map/ppermute | solution.py:28
  186.4 6.6 %collective-permute-start.29 = (f32[128,128]{0,1:T(8,128)S(1)}, f32[128,128]{0,1:T(8,128)S(1)}, u32[]{:S(2)}, u32[]{:S(2)}) collective-permute-start(f32[128,128]{0,1:T(8,128)S(1)} %collective-permute-done.28), channel_id=1, source_target_pairs={{1,0},{2,1},{3,2},{4,3},{5,4},{6,5},{7,6},{8,7},{9,8},{10,9},{11,1... | collective-permute-start | bytes 196616 | tf_op jit(solution)/shard_map/ppermute | solution.py:30
  211.5 196.4 %reduce-scatter.8.cloned.1.call-start = ((), (), s32[]{:S(2)}) async-start(), calls=%async_computation.5 | async-start | bytes 1114112 | tf_op jit(solution)/shard_map/reduce_scatter | solution.py:66
  270.8 6.4 %collective-permute-start.30 = (f32[128,128]{0,1:T(8,128)S(1)}, f32[128,128]{0,1:T(8,128)S(1)}, u32[]{:S(2)}, u32[]{:S(2)}) collective-permute-start(f32[128,128]{0,1:T(8,128)S(1)} %get-tuple-element.22), channel_id=1, source_target_pairs={{0,1},{1,2},{2,3},{3,4},{4,5},{5,6},{6,7},{7,8},{8,9},{9,10},{10,1... | collective-permute-start | bytes 196616 | tf_op jit(solution)/shard_map/ppermute | solution.py:28
  277.3 6.5 %collective-permute-start.31 = (f32[128,128]{0,1:T(8,128)S(1)}, f32[128,128]{0,1:T(8,128)S(1)}, u32[]{:S(2)}, u32[]{:S(2)}) collective-permute-start(f32[128,128]{0,1:T(8,128)S(1)} %collective-permute-done.30), channel_id=1, source_target_pairs={{0,1},{1,2},{2,3},{3,4},{4,5},{5,6},{6,7},{7,8},{8,9},{9,10},{10,1... | collective-permute-start | bytes 196616 | tf_op jit(solution)/shard_map/ppermute | solution.py:28
  277.3 6.5 %collective-permute-start.38 = (f32[128,128]{0,1:T(8,128)S(1)}, f32[128,128]{0,1:T(8,128)S(1)}, u32[]{:S(2)}, u32[]{:S(2)}) collective-permute-start(f32[128,128]{0,1:T(8,128)S(1)} %get-tuple-element.22), channel_id=1, source_target_pairs={{1,0},{2,1},{3,2},{4,3},{5,4},{6,5},{7,6},{8,7},{9,8},{10,9},{11,1... | collective-permute-start | bytes 196616 | tf_op jit(solution)/shard_map/ppermute | solution.py:30
  283.8 6.4 %collective-permute-start.32 = (f32[128,128]{0,1:T(8,128)S(1)}, f32[128,128]{0,1:T(8,128)S(1)}, u32[]{:S(2)}, u32[]{:S(2)}) collective-permute-start(f32[128,128]{0,1:T(8,128)S(1)} %collective-permute-done.31), channel_id=1, source_target_pairs={{0,1},{1,2},{2,3},{3,4},{4,5},{5,6},{6,7},{7,8},{8,9},{9,10},{10,1... | collective-permute-start | bytes 196616 | tf_op jit(solution)/shard_map/ppermute | solution.py:28
  283.8 6.4 %collective-permute-start.39 = (f32[128,128]{0,1:T(8,128)S(1)}, f32[128,128]{0,1:T(8,128)S(1)}, u32[]{:S(2)}, u32[]{:S(2)}) collective-permute-start(f32[128,128]{0,1:T(8,128)S(1)} %collective-permute-done.38), channel_id=1, source_target_pairs={{1,0},{2,1},{3,2},{4,3},{5,4},{6,5},{7,6},{8,7},{9,8},{10,9},{11,1... | collective-permute-start | bytes 196616 | tf_op jit(solution)/shard_map/ppermute | solution.py:30
  290.1 6.4 %collective-permute-start.33 = (f32[128,128]{0,1:T(8,128)S(1)}, f32[128,128]{0,1:T(8,128)S(1)}, u32[]{:S(2)}, u32[]{:S(2)}) collective-permute-start(f32[128,128]{0,1:T(8,128)S(1)} %collective-permute-done.32), channel_id=1, source_target_pairs={{0,1},{1,2},{2,3},{3,4},{4,5},{5,6},{6,7},{7,8},{8,9},{9,10},{10,1... | collective-permute-start | bytes 196616 | tf_op jit(solution)/shard_map/ppermute | solution.py:28
  290.1 6.4 %collective-permute-start.40 = (f32[128,128]{0,1:T(8,128)S(1)}, f32[128,128]{0,1:T(8,128)S(1)}, u32[]{:S(2)}, u32[]{:S(2)}) collective-permute-start(f32[128,128]{0,1:T(8,128)S(1)} %collective-permute-done.39), channel_id=1, source_target_pairs={{1,0},{2,1},{3,2},{4,3},{5,4},{6,5},{7,6},{8,7},{9,8},{10,9},{11,1... | collective-permute-start | bytes 196616 | tf_op jit(solution)/shard_map/ppermute | solution.py:30
  296.5 6.4 %collective-permute-start.34 = (f32[128,128]{0,1:T(8,128)S(1)}, f32[128,128]{0,1:T(8,128)S(1)}, u32[]{:S(2)}, u32[]{:S(2)}) collective-permute-start(f32[128,128]{0,1:T(8,128)S(1)} %collective-permute-done.33), channel_id=1, source_target_pairs={{0,1},{1,2},{2,3},{3,4},{4,5},{5,6},{6,7},{7,8},{8,9},{9,10},{10,1... | collective-permute-start | bytes 196616 | tf_op jit(solution)/shard_map/ppermute | solution.py:28
  296.6 6.4 %collective-permute-start.41 = (f32[128,128]{0,1:T(8,128)S(1)}, f32[128,128]{0,1:T(8,128)S(1)}, u32[]{:S(2)}, u32[]{:S(2)}) collective-permute-start(f32[128,128]{0,1:T(8,128)S(1)} %collective-permute-done.40), channel_id=1, source_target_pairs={{1,0},{2,1},{3,2},{4,3},{5,4},{6,5},{7,6},{8,7},{9,8},{10,9},{11,1... | collective-permute-start | bytes 196616 | tf_op jit(solution)/shard_map/ppermute | solution.py:30
  302.9 6.4 %collective-permute-start.35 = (f32[128,128]{0,1:T(8,128)S(1)}, f32[128,128]{0,1:T(8,128)S(1)}, u32[]{:S(2)}, u32[]{:S(2)}) collective-permute-start(f32[128,128]{0,1:T(8,128)S(1)} %collective-permute-done.34), channel_id=1, source_target_pairs={{0,1},{1,2},{2,3},{3,4},{4,5},{5,6},{6,7},{7,8},{8,9},{9,10},{10,1... | collective-permute-start | bytes 196616 | tf_op jit(solution)/shard_map/ppermute | solution.py:28
  302.9 6.4 %collective-permute-start.42 = (f32[128,128]{0,1:T(8,128)S(1)}, f32[128,128]{0,1:T(8,128)S(1)}, u32[]{:S(2)}, u32[]{:S(2)}) collective-permute-start(f32[128,128]{0,1:T(8,128)S(1)} %collective-permute-done.41), channel_id=1, source_target_pairs={{1,0},{2,1},{3,2},{4,3},{5,4},{6,5},{7,6},{8,7},{9,8},{10,9},{11,1... | collective-permute-start | bytes 196616 | tf_op jit(solution)/shard_map/ppermute | solution.py:30
  309.3 6.4 %collective-permute-start.36 = (f32[128,128]{0,1:T(8,128)S(1)}, f32[128,128]{0,1:T(8,128)S(1)}, u32[]{:S(2)}, u32[]{:S(2)}) collective-permute-start(f32[128,128]{0,1:T(8,128)S(1)} %collective-permute-done.35), channel_id=1, source_target_pairs={{0,1},{1,2},{2,3},{3,4},{4,5},{5,6},{6,7},{7,8},{8,9},{9,10},{10,1... | collective-permute-start | bytes 196616 | tf_op jit(solution)/shard_map/ppermute | solution.py:28
  309.3 6.4 %collective-permute-start.43 = (f32[128,128]{0,1:T(8,128)S(1)}, f32[128,128]{0,1:T(8,128)S(1)}, u32[]{:S(2)}, u32[]{:S(2)}) collective-permute-start(f32[128,128]{0,1:T(8,128)S(1)} %collective-permute-done.42), channel_id=1, source_target_pairs={{1,0},{2,1},{3,2},{4,3},{5,4},{6,5},{7,6},{8,7},{9,8},{10,9},{11,1... | collective-permute-start | bytes 196616 | tf_op jit(solution)/shard_map/ppermute | solution.py:30
  315.7 6.4 %collective-permute-start.37 = (f32[128,128]{0,1:T(8,128)S(1)}, f32[128,128]{0,1:T(8,128)S(1)}, u32[]{:S(2)}, u32[]{:S(2)}) collective-permute-start(f32[128,128]{0,1:T(8,128)S(1)} %collective-permute-done.36), channel_id=1, source_target_pairs={{0,1},{1,2},{2,3},{3,4},{4,5},{5,6},{6,7},{7,8},{8,9},{9,10},{10,1... | collective-permute-start | bytes 196616 | tf_op jit(solution)/shard_map/ppermute | solution.py:28
  315.7 15.8 %collective-permute-start.44 = (f32[128,128]{0,1:T(8,128)S(1)}, f32[128,128]{0,1:T(8,128)S(1)}, u32[]{:S(2)}, u32[]{:S(2)}) collective-permute-start(f32[128,128]{0,1:T(8,128)S(1)} %collective-permute-done.43), channel_id=1, source_target_pairs={{1,0},{2,1},{3,2},{4,3},{5,4},{6,5},{7,6},{8,7},{9,8},{10,9},{11,1... | collective-permute-start | bytes 196616 | tf_op jit(solution)/shard_map/ppermute | solution.py:30
  408.7 6.4 %collective-permute-start.45 = (f32[128,128]{0,1:T(8,128)S(1)}, f32[128,128]{0,1:T(8,128)S(1)}, u32[]{:S(2)}, u32[]{:S(2)}) collective-permute-start(f32[128,128]{0,1:T(8,128)S(1)} %get-tuple-element.20), channel_id=1, source_target_pairs={{0,1},{1,2},{2,3},{3,4},{4,5},{5,6},{6,7},{7,8},{8,9},{9,10},{10,1... | collective-permute-start | bytes 196616 | tf_op jit(solution)/shard_map/ppermute | solution.py:28
  415.2 6.5 %collective-permute-start.46 = (f32[128,128]{0,1:T(8,128)S(1)}, f32[128,128]{0,1:T(8,128)S(1)}, u32[]{:S(2)}, u32[]{:S(2)}) collective-permute-start(f32[128,128]{0,1:T(8,128)S(1)} %collective-permute-done.45), channel_id=1, source_target_pairs={{0,1},{1,2},{2,3},{3,4},{4,5},{5,6},{6,7},{7,8},{8,9},{9,10},{10,1... | collective-permute-start | bytes 196616 | tf_op jit(solution)/shard_map/ppermute | solution.py:28
  415.2 6.5 %collective-permute-start.53 = (f32[128,128]{0,1:T(8,128)S(1)}, f32[128,128]{0,1:T(8,128)S(1)}, u32[]{:S(2)}, u32[]{:S(2)}) collective-permute-start(f32[128,128]{0,1:T(8,128)S(1)} %get-tuple-element.20), channel_id=1, source_target_pairs={{1,0},{2,1},{3,2},{4,3},{5,4},{6,5},{7,6},{8,7},{9,8},{10,9},{11,1... | collective-permute-start | bytes 196616 | tf_op jit(solution)/shard_map/ppermute | solution.py:30
  421.7 6.4 %collective-permute-start.47 = (f32[128,128]{0,1:T(8,128)S(1)}, f32[128,128]{0,1:T(8,128)S(1)}, u32[]{:S(2)}, u32[]{:S(2)}) collective-permute-start(f32[128,128]{0,1:T(8,128)S(1)} %collective-permute-done.46), channel_id=1, source_target_pairs={{0,1},{1,2},{2,3},{3,4},{4,5},{5,6},{6,7},{7,8},{8,9},{9,10},{10,1... | collective-permute-start | bytes 196616 | tf_op jit(solution)/shard_map/ppermute | solution.py:28
  421.7 6.4 %collective-permute-start.54 = (f32[128,128]{0,1:T(8,128)S(1)}, f32[128,128]{0,1:T(8,128)S(1)}, u32[]{:S(2)}, u32[]{:S(2)}) collective-permute-start(f32[128,128]{0,1:T(8,128)S(1)} %collective-permute-done.53), channel_id=1, source_target_pairs={{1,0},{2,1},{3,2},{4,3},{5,4},{6,5},{7,6},{8,7},{9,8},{10,9},{11,1... | collective-permute-start | bytes 196616 | tf_op jit(solution)/shard_map/ppermute | solution.py:30
  428.1 6.4 %collective-permute-start.48 = (f32[128,128]{0,1:T(8,128)S(1)}, f32[128,128]{0,1:T(8,128)S(1)}, u32[]{:S(2)}, u32[]{:S(2)}) collective-permute-start(f32[128,128]{0,1:T(8,128)S(1)} %collective-permute-done.47), channel_id=1, source_target_pairs={{0,1},{1,2},{2,3},{3,4},{4,5},{5,6},{6,7},{7,8},{8,9},{9,10},{10,1... | collective-permute-start | bytes 196616 | tf_op jit(solution)/shard_map/ppermute | solution.py:28
  428.1 6.4 %collective-permute-start.55 = (f32[128,128]{0,1:T(8,128)S(1)}, f32[128,128]{0,1:T(8,128)S(1)}, u32[]{:S(2)}, u32[]{:S(2)}) collective-permute-start(f32[128,128]{0,1:T(8,128)S(1)} %collective-permute-done.54), channel_id=1, source_target_pairs={{1,0},{2,1},{3,2},{4,3},{5,4},{6,5},{7,6},{8,7},{9,8},{10,9},{11,1... | collective-permute-start | bytes 196616 | tf_op jit(solution)/shard_map/ppermute | solution.py:30
  434.5 6.5 %collective-permute-start.49 = (f32[128,128]{0,1:T(8,128)S(1)}, f32[128,128]{0,1:T(8,128)S(1)}, u32[]{:S(2)}, u32[]{:S(2)}) collective-permute-start(f32[128,128]{0,1:T(8,128)S(1)} %collective-permute-done.48), channel_id=1, source_target_pairs={{0,1},{1,2},{2,3},{3,4},{4,5},{5,6},{6,7},{7,8},{8,9},{9,10},{10,1... | collective-permute-start | bytes 196616 | tf_op jit(solution)/shard_map/ppermute | solution.py:28
  434.5 7.1 %collective-permute-start.56 = (f32[128,128]{0,1:T(8,128)S(1)}, f32[128,128]{0,1:T(8,128)S(1)}, u32[]{:S(2)}, u32[]{:S(2)}) collective-permute-start(f32[128,128]{0,1:T(8,128)S(1)} %collective-permute-done.55), channel_id=1, source_target_pairs={{1,0},{2,1},{3,2},{4,3},{5,4},{6,5},{7,6},{8,7},{9,8},{10,9},{11,1... | collective-permute-start | bytes 196616 | tf_op jit(solution)/shard_map/ppermute | solution.py:30
  441.0 6.4 %collective-permute-start.50 = (f32[128,128]{0,1:T(8,128)S(1)}, f32[128,128]{0,1:T(8,128)S(1)}, u32[]{:S(2)}, u32[]{:S(2)}) collective-permute-start(f32[128,128]{0,1:T(8,128)S(1)} %collective-permute-done.49), channel_id=1, source_target_pairs={{0,1},{1,2},{2,3},{3,4},{4,5},{5,6},{6,7},{7,8},{8,9},{9,10},{10,1... | collective-permute-start | bytes 196616 | tf_op jit(solution)/shard_map/ppermute | solution.py:28
  441.6 44.9 %collective-permute-start.57 = (f32[128,128]{0,1:T(8,128)S(1)}, f32[128,128]{0,1:T(8,128)S(1)}, u32[]{:S(2)}, u32[]{:S(2)}) collective-permute-start(f32[128,128]{0,1:T(8,128)S(1)} %collective-permute-done.56), channel_id=1, source_target_pairs={{1,0},{2,1},{3,2},{4,3},{5,4},{6,5},{7,6},{8,7},{9,8},{10,9},{11,1... | collective-permute-start | bytes 196616 | tf_op jit(solution)/shard_map/ppermute | solution.py:30
  447.3 39.1 %collective-permute-start.51 = (f32[128,128]{0,1:T(8,128)S(1)}, f32[128,128]{0,1:T(8,128)S(1)}, u32[]{:S(2)}, u32[]{:S(2)}) collective-permute-start(f32[128,128]{0,1:T(8,128)S(1)} %collective-permute-done.50), channel_id=1, source_target_pairs={{0,1},{1,2},{2,3},{3,4},{4,5},{5,6},{6,7},{7,8},{8,9},{9,10},{10,1... | collective-permute-start | bytes 196616 | tf_op jit(solution)/shard_map/ppermute | solution.py:28
  486.4 2.4 collective-permute-start.58
  486.5 6.5 %collective-permute-start.52 = (f32[128,128]{0,1:T(8,128)S(1)}, f32[128,128]{0,1:T(8,128)S(1)}, u32[]{:S(2)}, u32[]{:S(2)}) collective-permute-start(f32[128,128]{0,1:T(8,128)S(1)} %collective-permute-done.51), channel_id=1, source_target_pairs={{0,1},{1,2},{2,3},{3,4},{4,5},{5,6},{6,7},{7,8},{8,9},{9,10},{10,1... | collective-permute-start | bytes 196616 | tf_op jit(solution)/shard_map/ppermute | solution.py:28
  488.8 5.9 %collective-permute-start.59 = (f32[128,128]{0,1:T(8,128)S(1)}, f32[128,128]{0,1:T(8,128)S(1)}, u32[]{:S(2)}, u32[]{:S(2)}) collective-permute-start(f32[128,128]{0,1:T(8,128)S(1)} %collective-permute-done.58), channel_id=1, source_target_pairs={{1,0},{2,1},{3,2},{4,3},{5,4},{6,5},{7,6},{8,7},{9,8},{10,9},{11,1... | collective-permute-start | bytes 196616 | tf_op jit(solution)/shard_map/ppermute | solution.py:30
  (2 other events, 36.4 us)
Sparse Core Ops, SparseCore 0:
  81.5 59.0 reduce-scatter.3
  211.6 58.3 reduce-scatter.5
  353.2 54.6 reduce-scatter.7
